TPU v7x, 256 devices: a whole 4x4x8 slice. The times are simulated.
256 devices in a mesh: ctx: 16 (over y, x), head: 16 (over z, core).
Axes of the slice: x: 4, y: 4, z: 8, core: 2. Of those that a mesh axis runs over, the one named last changes fastest.
Arguments:
- queries: bfloat16 [2, 4096, 8192], P(None, 'ctx', 'head'), may hold values from -4.5 to 4.5
- key_rows: bfloat16 [2, 4096, 512], P(None, 'ctx'), may hold values from -4.5 to 4.5
- value_rows: bfloat16 [2, 4096, 512], P(None, 'ctx'), may hold values from -6 to 6
- out_weight: bfloat16 [8192, 8192], P('head'), may hold values from -0.0625 to 0.0625
- span_owner: int32 [2, 16], replicated, may hold values from 0 to 15, each once within a row
- vertical_blocks: int32 [64, 4], replicated, may hold values from 0 to 63, as said below
- slash_offsets: int32 [64, 4], replicated, may hold values from 1 to 63, as said below
Outputs:
- projected: bfloat16 [2, 4096, 8192], P(None, ('ctx', 'head'))
Inputs may be any that keep to these rules, and one draw needn't show every extreme that they name: `vertical_blocks`: the 4 entries of a head are distinct block numbers. `slash_offsets`: the 4 entries of a head are distinct.
All inputs are finite; a program needn't handle non-finite values.
Results may differ from a plain program's by a relative error of at most 0.017.
Values may be sent and summed in bfloat16 or wider, within the bound.
No kernel may reach another device: no remote copies, remote signals or barrier semaphores. Data moves between devices by JAX's collectives and lax.ppermute only.
A program may use at most 64 MiB of HBM per device.

v0:
```python
import math
import jax
import jax.numpy as jnp
from jax import lax
from jax.sharding import PartitionSpec as P

QH = 64
KVH = 4
HD = 128
BLK = 128
STEPS = 2


def tile_blocks(block_ids, vertical, slanted, owner_flat, span_blocks, span_count):
    column = block_ids[:, None]
    vert_rows = jnp.broadcast_to(vertical[None, :], (block_ids.shape[0], vertical.shape[0]))
    slash_rows = column - slanted[None, :]
    vert_valid = vert_rows < column
    repeated = jnp.any(slash_rows[:, :, None] == vertical[None, None, :], axis=2)
    slash_valid = (slash_rows >= 0) & jnp.logical_not(repeated)
    chosen = jnp.concatenate([column, vert_rows, slash_rows], axis=1)
    allowed = jnp.concatenate([jnp.ones_like(column, dtype=bool), vert_valid, slash_valid], axis=1)
    chosen = jnp.where(allowed, chosen, column)
    span_index = chosen // span_blocks
    slot_ids = jnp.arange(owner_flat.shape[0], dtype=jnp.int32)
    holder = jnp.sum(
        jnp.where(span_index[:, :, None] == slot_ids[None, None, :], owner_flat[None, None, :], 0),
        axis=2,
    )
    step_index = span_index // span_count
    stored = (step_index * span_count + holder) * span_blocks + chosen % span_blocks
    return (stored, allowed)


def block_mask(allowed, block_rows):
    positions = jnp.arange(block_rows, dtype=jnp.int32)
    causal = positions[None, :] <= positions[:, None]
    tile_count = allowed.shape[1]
    first_tile = jnp.arange(tile_count, dtype=jnp.int32) == 0
    inside = causal[None, :, None, :] | jnp.logical_not(first_tile)[None, None, :, None]
    visible = allowed[:, None, :, None] & inside
    return visible.reshape(allowed.shape[0], block_rows, tile_count * block_rows)


def attend_tiles(query_tile_set, key_store, value_store, stored, allowed):
    block_count = stored.shape[0]
    tile_count = stored.shape[1]
    block_rows = query_tile_set.shape[1]
    head_features = query_tile_set.shape[2]
    key_tile_set = jnp.take(key_store, stored.reshape(-1), axis=0).reshape(
        block_count, tile_count * block_rows, head_features
    )
    value_tile_set = jnp.take(value_store, stored.reshape(-1), axis=0).reshape(
        block_count, tile_count * block_rows, head_features
    )
    logit_scores = jnp.einsum(
        "zcs,zvs->zcv", query_tile_set, key_tile_set, preferred_element_type=jnp.float32
    ) * (1.0 / math.sqrt(head_features))
    logit_scores = jnp.where(block_mask(allowed, block_rows), logit_scores, -jnp.inf)
    largest = jnp.max(logit_scores, axis=2, keepdims=True)
    weights = jnp.exp(logit_scores - largest)
    totals = jnp.sum(weights, axis=2, keepdims=True)
    mixed_output = jnp.einsum(
        "ynj,yjw->ynw",
        weights.astype(jnp.bfloat16),
        value_tile_set,
        preferred_element_type=jnp.float32,
    )
    return (mixed_output / totals).astype(jnp.bfloat16)


def local(queries, key_rows, value_rows, out_weight, span_owner, vertical_blocks, slash_offsets):
    local_heads = queries.shape[2] // HD
    span_rows = queries.shape[1]
    span_blocks = span_rows // BLK
    span_count = lax.axis_size("ctx")
    head_groups = lax.axis_size("head")
    rows_share = span_rows // head_groups
    first_head = lax.axis_index("head") * local_heads
    kv_head = first_head // (QH // KVH)
    vertical = lax.dynamic_slice_in_dim(vertical_blocks, first_head, local_heads, 0)
    slanted = lax.dynamic_slice_in_dim(slash_offsets, first_head, local_heads, 0)
    own_keys = lax.dynamic_slice_in_dim(key_rows, kv_head * HD, HD, 2)
    own_values = lax.dynamic_slice_in_dim(value_rows, kv_head * HD, HD, 2)
    paired = jnp.stack([own_keys, own_values], axis=1)
    owner_flat = span_owner.reshape(-1)
    device = lax.axis_index("ctx")
    device_ids = jnp.arange(span_count, dtype=jnp.int32)
    places = jnp.sum(device_ids[None, :] * (span_owner == device).astype(jnp.int32), axis=1)
    tiler = jax.vmap(tile_blocks, in_axes=(None, 0, 0, None, None, None))
    gathered = lax.all_gather(paired, "ctx", axis=2, tiled=True)
    outputs = []
    for current in range(STEPS):
        kv_store = gathered[: current + 1]
        key_store = kv_store[:, 0].reshape(-1, BLK, HD)
        value_store = kv_store[:, 1].reshape(-1, BLK, HD)
        block_ids = (current * span_count + places[current]) * span_blocks + jnp.arange(
            span_blocks, dtype=jnp.int32
        )
        stored, allowed = tiler(block_ids, vertical, slanted, owner_flat, span_blocks, span_count)
        stored = stored.reshape(local_heads * span_blocks, -1)
        allowed = allowed.reshape(local_heads * span_blocks, -1)
        query_tile_set = (
            queries[current]
            .reshape(span_blocks, BLK, local_heads, HD)
            .transpose(2, 0, 1, 3)
            .reshape(local_heads * span_blocks, BLK, HD)
        )
        result_tiles = attend_tiles(query_tile_set, key_store, value_store, stored, allowed)
        attended = (
            result_tiles.reshape(local_heads, span_blocks, BLK, HD)
            .transpose(1, 2, 0, 3)
            .reshape(span_rows, local_heads * HD)
        )
        outputs.append(attended)
    arranged = (
        jnp.stack(outputs)
        .reshape(STEPS, head_groups, rows_share, -1)
        .transpose(1, 0, 2, 3)
        .reshape(STEPS * span_rows, -1)
    )
    summed = lax.psum_scatter(
        jnp.dot(arranged, out_weight, preferred_element_type=jnp.float32).astype(jnp.bfloat16),
        "head",
        scatter_dimension=0,
        tiled=True,
    ).astype(jnp.float32)
    return summed.reshape(STEPS, rows_share, -1).astype(jnp.bfloat16)


def solution(mesh):
    in_specs = (
        P(None, "ctx", "head"),
        P(None, "ctx", None),
        P(None, "ctx", None),
        P("head", None),
        P(),
        P(),
        P(),
    )
    out_specs = P(None, ("ctx", "head"), None)
    return jax.shard_map(local, mesh=mesh, in_specs=in_specs, out_specs=out_specs, check_vma=False)
```

profile of v0, /device:TPU:2, one launch (start us, length us, event | category | flops | bytes accessed | tf_op | source)
XLA Modules:
  0.0 190.6 jit_solution(16768299913413299130)
XLA Ops:
  6.5 1.0 dynamic-slice_bitcast_fusion
  7.5 0.7 pad_maximum_fusion
  8.3 0.0 all-gather.2.cloned.1.call-update
  8.3 0.0 reduce-scatter.2.cloned.1.call-start
  8.3 0.8 broadcast_in_dim_reshape.2
  9.1 0.1 constant_dynamic-slice_fusion
  9.2 0.1 copy.38
  9.3 0.8 fusion.26
  10.1 0.6 fusion.33
  11.9 0.8 constant_dynamic-slice_fusion.1
  12.7 0.1 copy.37
  12.8 0.1 broadcast_subtract_fusion
  12.9 0.4 compare_reduce_fusion.1
  13.3 0.1 fusion.32
  13.4 0.1 broadcast_in_dim.106
  13.5 0.1 broadcast_in_dim.62
  13.6 0.1 and_select_fusion
  13.7 0.1 copy.43
  13.8 0.1 copy.51
  13.9 0.8 select_reduce_fusion.1
  14.6 0.1 copy.52
  14.7 0.1 reduce_sum.54
  14.8 0.1 select_n.118
  14.9 0.1 copy.44
  15.0 0.1 reduce_sum.51
  15.1 0.1 select_n.110
  15.2 1.1 fusion.31
  16.3 0.1 reshape_squeeze.22
  16.4 0.1 lt.82
  16.5 0.1 lt.90
  16.6 0.1 fusion.24
  16.7 0.1 add_bitcast_fusion
  16.8 0.1 copy.50
  16.9 0.1 reshape_squeeze.19
  16.9 0.8 copy.45
  17.7 0.1 copy.42
  17.8 0.1 broadcast_bitcast_fusion.2
  17.9 0.2 bitcast_or_fusion
  18.2 0.1 broadcast_bitcast_fusion
  18.3 0.1 broadcast_bitcast_fusion.1
  18.4 50.8 %all-gather.2.cloned.1.call-done = bf16[2,2,4096,128]{3,2,0,1:T(8,128)(2,1)} async-done(((bf16[2,2,256,128]{3,2,0,1:T(8,128)(2,1)}), bf16[2,2,4096,128]{3,2,0,1:T(8,128)(2,1)}) %all-gather.2.cloned.1.call-update) | async-done | bytes 4194320 | tf_op jit(solution)/shard_map/all_gather | solution.py:91
  69.2 3.8 %fusion.30 = (bf16[2,1,4096,128]{3,2,0,1:T(8,128)(2,1)}, bf16[2,1,4096,128]{3,2,0,1:T(8,128)(2,1)S(1)}) fusion(bf16[2,2,4096,128]{3,2,0,1:T(8,128)(2,1)} %all-gather.2.cloned.1.call-done), kind=kLoop, calls=%fused_computation.106 | loop fusion | bytes 8388608 | tf_op jit(solution)/shard_map/slice | solution.py:95
  73.0 4.0 %gather_fusion.2 = bf16[72,128,128]{2,1,0:T(8,128)(2,1)} fusion(bf16[64,128,128]{2,1,0:T(8,128)(2,1)} %bitcast.63, s32[1024]{0:T(1024)S(1)} %pad_clamp_fusion), kind=kCustom, calls=%fused_computation.1.clone | custom fusion | bytes 4718880 | tf_op jit(solution)/shard_map/jit(_take)/gather | solution.py:50
  77.1 2.5 %gather_fusion.3 = bf16[72,128,128]{2,1,0:T(8,128)(2,1)} fusion(bf16[64,128,128]{2,1,0:T(8,128)(2,1)S(1)} %bitcast.62, s32[1024]{0:T(1024)S(1)} %pad_clamp_fusion), kind=kCustom, calls=%fused_computation.3.clone | custom fusion | bytes 4718880 | tf_op jit(solution)/shard_map/jit(_take)/gather | solution.py:53
  79.5 2.9 %broadcast_select_fusion.1 = (bf16[72,128,128]{2,1,0:T(8,128)(2,1)S(1)}, bf16[72,128,128]{2,1,0:T(8,128)(2,1)S(1)}) fusion(bf16[72,128,128]{2,1,0:T(8,128)(2,1)} %gather_fusion.2, pred[72]{0:T(512)(128)(4,1)S(1)} %get-tuple-element.13, bf16[72,128,128]{2,1,0:T(8,128)(2,1)} %gather_fusion.3), kind=kLoop, calls=%fused_computation.20 | loop fusion | flops 2359296 | bytes 9437256 | tf_op jit(solution)/shard_map/jit(_take)/select_n | solution.py:50
  82.4 3.2 %fusion.34 = (f32[8,128]{1,0:T(8,128)S(1)}, f32[8,128,1152]{1,2,0:T(8,128)S(1)}) fusion(bf16[8,1152,128]{2,1,0:T(8,128)(2,1)S(1)} %bitcast.67, bf16[8,128,128]{2,1,0:T(8,128)(2,1)S(1)} %bitcast.73, pred[128,1152]{0,1:T(8,128)(4,1)S(1)} %bitcast_or_fusion, pred[8,1152]{1,0:T(8,128)(4,1)S(1)} %broadcast_bitcast_fusion), kind=kOutput, calls=%fused_computation.110 | convolution fusion | flops 306707456 | bytes 7500800 | tf_op jit(solution)/shard_map/zcs,zvs->zcv/dot_general | solution.py:56
  85.6 0.6 fusion.2
  86.2 1.3 fusion.19
  87.5 0.2 copy.63
  87.7 0.8 stack.20
  88.5 1.7 fusion.29
  90.2 2.4 %gather_fusion = bf16[72,128,128]{2,1,0:T(8,128)(2,1)} fusion(bf16[32,128,128]{2,1,0:T(8,128)(2,1)S(1)} %bitcast.61, s32[1024]{0:T(1024)S(1)} %pad_clamp_fusion.1), kind=kCustom, calls=%fused_computation.clone | custom fusion | bytes 4718880 | tf_op jit(solution)/shard_map/jit(_take)/gather | solution.py:50
  92.6 2.4 %gather_fusion.1 = bf16[72,128,128]{2,1,0:T(8,128)(2,1)} fusion(bf16[32,128,128]{2,1,0:T(8,128)(2,1)S(1)} %bitcast.60, s32[1024]{0:T(1024)S(1)} %pad_clamp_fusion.1), kind=kCustom, calls=%fused_computation.2.clone | custom fusion | bytes 4718880 | tf_op jit(solution)/shard_map/jit(_take)/gather | solution.py:53
  95.0 2.4 %broadcast_select_fusion.3 = (bf16[72,128,128]{2,1,0:T(8,128)(2,1)S(1)}, bf16[72,128,128]{2,1,0:T(8,128)(2,1)S(1)}) fusion(bf16[72,128,128]{2,1,0:T(8,128)(2,1)S(1)} %copy-done.1, pred[72]{0:T(512)(128)(4,1)S(1)} %get-tuple-element.55, bf16[72,128,128]{2,1,0:T(8,128)(2,1)} %gather_fusion.1), kind=kLoop, calls=%fused_computation.22 | loop fusion | flops 2359296 | bytes 9437256 | tf_op jit(solution)/shard_map/jit(_take)/select_n | solution.py:50
  97.5 2.9 %fusion.35 = (f32[8,128]{1,0:T(8,128)S(1)}, f32[8,128,1152]{1,2,0:T(8,128)S(1)}) fusion(bf16[8,1152,128]{2,1,0:T(8,128)(2,1)S(1)} %bitcast.66, bf16[8,128,128]{2,1,0:T(8,128)(2,1)S(1)} %bitcast.74, pred[128,1152]{0,1:T(8,128)(4,1)S(1)} %copy-done.5, pred[8,1152]{1,0:T(8,128)(4,1)S(1)} %broadcast_bitcast_fusion.1), kind=kOutput, calls=%fused_computation.111 | convolution fusion | flops 306707456 | bytes 7500800 | tf_op jit(solution)/shard_map/zcs,zvs->zcv/dot_general | solution.py:56
  100.4 0.6 fusion
  101.0 0.0 copy-start.2
  101.0 1.3 fusion.13
  102.3 0.2 copy.64
  102.5 0.1 stack.19
  102.6 0.1 maximum_bitcast_fusion
  102.7 10.2 %convolution_convert_fusion = bf16[512,8192]{1,0:T(8,128)(2,1)} fusion(bf16[512,512]{1,0:T(8,128)(2,1)S(1)} %bitcast.72, bf16[512,8192]{1,0:T(8,128)(2,1)} %param.14), kind=kOutput, calls=%fused_computation.4 | convolution fusion | flops 4299161600 | bytes 17301504 | tf_op jit(solution)/shard_map/dot_general | solution.py:123
  113.0 0.0 reduce-scatter.2.cloned.1.call-update
  113.0 70.7 %reduce-scatter.2.cloned.1.call-done = bf16[32,8192]{1,0:T(8,128)(2,1)} async-done(((bf16[512,8192]{1,0:T(8,128)(2,1)}), bf16[32,8192]{1,0:T(8,128)(2,1)}) %reduce-scatter.2.cloned.1.call-update) | async-done | bytes 524304 | tf_op jit(solution)/shard_map/reduce_scatter | solution.py:122
  (28 shorter events, 0.2 us)
Async XLA Ops:
  6.5 2.6 %copy-start = (s32[64,4]{0,1:T(4,128)S(1)}, s32[64,4]{0,1:T(4,128)}, u32[]{:S(2)}) copy-start(s32[64,4]{0,1:T(4,128)} %param.17) | copy-start | bytes 3076
  6.5 62.6 %all-gather.2.cloned.1.call-start = ((), (), s32[]{:S(2)}) async-start(), calls=%async_computation.1 | async-start | bytes 4456448 | tf_op jit(solution)/shard_map/all_gather | solution.py:91
  8.3 175.4 %reduce-scatter.2.cloned.1.call-start = ((), (), s32[]{:S(2)}) async-start(), calls=%async_computation.2 | async-start | bytes 8912896 | tf_op jit(solution)/shard_map/reduce_scatter | solution.py:122
  18.1 64.3 %copy-start.4 = (pred[128,1152]{0,1:T(8,128)(4,1)}, pred[128,1152]{0,1:T(8,128)(4,1)S(1)}, u32[]{:S(2)}) copy-start(pred[128,1152]{0,1:T(8,128)(4,1)S(1)} %bitcast_or_fusion) | copy-start | bytes 442372
  92.6 2.4 %copy-start.1 = (bf16[72,128,128]{2,1,0:T(8,128)(2,1)S(1)}, bf16[72,128,128]{2,1,0:T(8,128)(2,1)}, u32[]{:S(2)}) copy-start(bf16[72,128,128]{2,1,0:T(8,128)(2,1)} %gather_fusion) | copy-start | bytes 7077892
  95.0 2.4 %copy-start.3 = (bf16[2,128,4,128]{3,1,0,2:T(8,128)(2,1)S(1)}, bf16[2,128,4,128]{3,1,0,2:T(8,128)(2,1)}, u32[]{:S(2)}) copy-start(bf16[2,128,4,128]{3,1,0,2:T(8,128)(2,1)} %copy.45) | copy-start | bytes 786436
  95.0 2.4 %copy-start.5 = (pred[128,1152]{0,1:T(8,128)(4,1)S(1)}, pred[128,1152]{0,1:T(8,128)(4,1)}, u32[]{:S(2)}) copy-start(pred[128,1152]{0,1:T(8,128)(4,1)} %copy-done.4) | copy-start | bytes 442372
  101.0 1.6 copy-start.2
Sparse Core Ops, SparseCore 0:
  9.8 59.3 all-gather.1
  113.1 70.5 reduce-scatter.1
where the time goes:
time: 191 us
  waiting for transfers between devices  122 us (64%)
  local copies, waits for them, and re-layouts  25.2 us (13%)
  matrix products  18.8 us (10%)
  between operations  14.9 us (8%)
  other arithmetic  9.99 us (5%)
    reduce_scatter x1, waiting for transfers between devices, local(): lax.psum_scatter(jnp.dot(arranged, out_weight, preferred_element_type=jnp...  70.7 us
    all_gather x1, waiting for transfers between devices, local(): gathered = lax.all_gather(paired, 'ctx', axis=2, tiled=True)  50.8 us
    dot_general x1, matrix products, local(): jnp.dot(arranged, out_weight, preferred_element_type=jnp.float32)  10.2 us
    gather x2, local copies, waits for them, and re-layouts, attend_tiles(): jnp.take(key_store, stored.reshape(-1), axis=0)  6.48 us
    dot_general x2, matrix products, attend_tiles(): jnp.einsum('zcs,zvs->zcv', query_tile_set, key_tile_set, preferred_elemen...  6.08 us
    slice x2, local copies, waits for them, and re-layouts, local(): key_store = kv_store[:, 0].reshape(-1, BLK, HD)  5.51 us
    select_n x2, other arithmetic, attend_tiles(): jnp.take(key_store, stored.reshape(-1), axis=0)  5.24 us
    gather x2, local copies, waits for them, and re-layouts, attend_tiles(): jnp.take(value_store, stored.reshape(-1), axis=0)  4.91 us
  transfers between devices with their start and end apart: 2, of which 2 were waited for; matrix products, arithmetic and copies ran while one was open for 5% of the time, Pallas kernels for 0%

commit v1 on v0

--- a/solution.py
+++ b/solution.py
@@ -88,7 +88,9 @@
     device_ids = jnp.arange(span_count, dtype=jnp.int32)
     places = jnp.sum(device_ids[None, :] * (span_owner == device).astype(jnp.int32), axis=1)
     tiler = jax.vmap(tile_blocks, in_axes=(None, 0, 0, None, None, None))
-    gathered = lax.all_gather(paired, "ctx", axis=2, tiled=True)
+    gathered = jnp.concatenate(
+        lax.all_to_all(jnp.stack([paired] * lax.axis_size("ctx")), "ctx", 0, 0), axis=2
+    )
     outputs = []
     for current in range(STEPS):
         kv_store = gathered[: current + 1]

time: 191 us -> 205 us (1.073)
  starting transfers between devices: 0.04 us -> 7.65 us
  waiting for transfers between devices: 122 us -> 127 us
  local copies, waits for them, and re-layouts: 25.2 us -> 27.3 us
    all_to_all x0 -> x1, waiting for transfers between devices: none -> 52.2 us  [local(): lax.all_to_all(jnp.stack([paired] * lax.axis_size('ctx')), 'ctx', 0, 0)]
    all_gather x1 -> x0, waiting for transfers between devices: 50.8 us -> none  [local(): gathered = lax.all_gather(paired, 'ctx', axis=2, tiled=True)]
    all_to_all x0 -> x1, starting transfers between devices: none -> 7.61 us  [local(): lax.all_to_all(jnp.stack([paired] * lax.axis_size('ctx')), 'ctx', 0, 0)]
    reduce_scatter x1, waiting for transfers between devices: 70.7 us -> 75.1 us  [local(): lax.psum_scatter(jnp.dot(arranged, out_weight, preferred_element_type=jnp...]
    slice x2, local copies, waits for them, and re-layouts: 5.51 us -> 1.94 us  [local(): key_store = kv_store[:, 0].reshape(-1, BLK, HD)]
    another operation x0 -> x1, local copies, waits for them, and re-layouts: none -> 3 us  [local(): jnp.stack([paired] * lax.axis_size('ctx'))]
    all_to_all x0 -> x1, local copies, waits for them, and re-layouts: none -> 2.46 us  [local(): lax.all_to_all(jnp.stack([paired] * lax.axis_size('ctx')), 'ctx', 0, 0)]
  transfers between devices with their start and end apart: 2 -> 2, of which waited for: 2 -> 2; matrix products, arithmetic and copies ran while one was open for 5% -> 3% of each run, Pallas kernels for 0% -> 0%
where the time goes in v1:
time: 205 us
  waiting for transfers between devices  127 us (62%)
  local copies, waits for them, and re-layouts  27.3 us (13%)
  matrix products  18.8 us (9%)
  between operations  14.9 us (7%)
  other arithmetic  8.63 us (4%)
  starting transfers between devices  7.65 us (4%)
    reduce_scatter x1, waiting for transfers between devices, local(): lax.psum_scatter(jnp.dot(arranged, out_weight, preferred_element_type=jnp...  75.1 us
    all_to_all x1, waiting for transfers between devices, local(): lax.all_to_all(jnp.stack([paired] * lax.axis_size('ctx')), 'ctx', 0, 0)  52.2 us
    dot_general x1, matrix products, local(): jnp.dot(arranged, out_weight, preferred_element_type=jnp.float32)  10.2 us
    all_to_all x1, starting transfers between devices, local(): lax.all_to_all(jnp.stack([paired] * lax.axis_size('ctx')), 'ctx', 0, 0)  7.61 us
    gather x2, local copies, waits for them, and re-layouts, attend_tiles(): jnp.take(key_store, stored.reshape(-1), axis=0)  6.5 us
    dot_general x2, matrix products, attend_tiles(): jnp.einsum('zcs,zvs->zcv', query_tile_set, key_tile_set, preferred_elemen...  6.06 us
    select_n x2, other arithmetic, attend_tiles(): jnp.take(key_store, stored.reshape(-1), axis=0)  5.24 us
    gather x2, local copies, waits for them, and re-layouts, attend_tiles(): jnp.take(value_store, stored.reshape(-1), axis=0)  4.92 us
  transfers between devices with their start and end apart: 2, of which 2 were waited for; matrix products, arithmetic and copies ran while one was open for 3% of the time, Pallas kernels for 0%

profile of v1, /device:TPU:2, one launch (start us, length us, event | category | flops | bytes accessed | tf_op | source)
XLA Modules:
  0.0 204.6 jit_solution(4407788913346611130)
XLA Ops:
  6.5 1.0 dynamic-slice_bitcast_fusion
  7.6 3.0 %stack.17 = bf16[16,2,2,256,128]{4,3,2,1,0:T(8,128)(2,1)} broadcast(bf16[2,2,256,128]{3,2,1,0:T(8,128)(2,1)S(1)} %pad_maximum_fusion), dimensions={1,2,3,4} | broadcast | bytes 4456448 | tf_op jit(solution)/shard_map/stack | solution.py:92
  10.6 7.6 %all-to-all-start = ((bf16[16,2,2,256,128]{4,3,2,1,0:T(8,128)(2,1)}), bf16[16,2,2,256,128]{4,3,2,1,0:T(8,128)(2,1)}, u32[]{:S(2)}, u32[]{:S(2)}) async-start(bf16[16,2,2,256,128]{4,3,2,1,0:T(8,128)(2,1)} %stack.17), calls=%async_computation | async-start | bytes 8388608 | tf_op jit(solution)/shard_map/all_to_all | solution.py:92
  18.2 0.0 reduce-scatter.2.cloned.1.call-start
  18.3 0.1 broadcast_in_dim_reshape.2
  18.3 0.1 constant_dynamic-slice_fusion
  18.4 0.1 copy.55
  18.5 0.1 fusion.26
  18.6 0.6 fusion.33
  20.4 0.1 constant_dynamic-slice_fusion.1
  20.5 0.1 copy.54
  20.6 0.1 broadcast_subtract_fusion
  20.7 0.4 compare_reduce_fusion.1
  21.1 0.1 fusion.32
  21.2 0.1 broadcast_in_dim.106
  21.3 0.1 broadcast_in_dim.62
  21.4 0.1 and_select_fusion
  21.5 0.1 copy.60
  21.6 0.1 copy.69
  21.7 0.8 select_reduce_fusion.1
  22.5 0.1 copy.70
  22.6 0.1 reduce_sum.54
  22.6 0.1 select_n.118
  22.7 0.1 copy.61
  22.8 0.1 reduce_sum.51
  22.9 0.1 select_n.110
  23.1 0.1 reshape_squeeze.22
  23.2 0.1 lt.82
  23.3 0.1 lt.90
  23.4 0.1 fusion.24
  23.5 0.1 add_bitcast_fusion
  23.6 0.1 copy.68
  23.7 0.1 reshape_squeeze.19
  23.7 0.8 copy.63
  24.5 0.1 copy.59
  24.6 0.1 broadcast_bitcast_fusion.2
  24.7 0.2 bitcast_or_fusion
  25.0 0.1 broadcast_bitcast_fusion
  25.1 0.1 broadcast_bitcast_fusion.1
  25.1 52.2 %all-to-all-done = bf16[16,2,2,256,128]{4,3,2,1,0:T(8,128)(2,1)} async-done(((bf16[16,2,2,256,128]{4,3,2,1,0:T(8,128)(2,1)}), bf16[16,2,2,256,128]{4,3,2,1,0:T(8,128)(2,1)}, u32[]{:S(2)}, u32[]{:S(2)}) %all-to-all-start) | async-done | bytes 4194336 | tf_op jit(solution)/shard_map/all_to_all | solution.py:92
  77.4 2.5 %copy.85 = bf16[16,2,2,256,128]{4,3,0,2,1:T(8,128)(2,1)S(1)} copy(bf16[16,2,2,256,128]{4,3,2,1,0:T(8,128)(2,1)} %all-to-all-done) | data formatting | bytes 8388608 | tf_op jit(solution)/shard_map/all_to_all | solution.py:92
  79.9 1.8 fusion.29
  81.7 0.8 copy-done.2
  82.5 4.1 %gather_fusion.2 = bf16[72,128,128]{2,1,0:T(8,128)(2,1)} fusion(bf16[64,128,128]{2,1,0:T(8,128)(2,1)} %bitcast.71, s32[1024]{0:T(1024)S(1)} %pad_clamp_fusion), kind=kCustom, calls=%fused_computation.1.clone | custom fusion | bytes 4718880 | tf_op jit(solution)/shard_map/jit(_take)/gather | solution.py:50
  86.5 2.5 %gather_fusion.3 = bf16[72,128,128]{2,1,0:T(8,128)(2,1)} fusion(bf16[64,128,128]{2,1,0:T(8,128)(2,1)S(1)} %bitcast.70, s32[1024]{0:T(1024)S(1)} %pad_clamp_fusion), kind=kCustom, calls=%fused_computation.3.clone | custom fusion | bytes 4718880 | tf_op jit(solution)/shard_map/jit(_take)/gather | solution.py:53
  89.0 2.9 %broadcast_select_fusion.1 = (bf16[72,128,128]{2,1,0:T(8,128)(2,1)S(1)}, bf16[72,128,128]{2,1,0:T(8,128)(2,1)S(1)}) fusion(bf16[72,128,128]{2,1,0:T(8,128)(2,1)} %gather_fusion.2, pred[72]{0:T(512)(128)(4,1)S(1)} %get-tuple-element.13, bf16[72,128,128]{2,1,0:T(8,128)(2,1)} %gather_fusion.3), kind=kLoop, calls=%fused_computation.20 | loop fusion | flops 2359296 | bytes 9437256 | tf_op jit(solution)/shard_map/jit(_take)/select_n | solution.py:50
  91.9 3.1 %fusion.34 = (f32[8,128]{1,0:T(8,128)S(1)}, f32[8,128,1152]{1,2,0:T(8,128)S(1)}) fusion(bf16[8,1152,128]{2,1,0:T(8,128)(2,1)S(1)} %bitcast.76, bf16[8,128,128]{2,1,0:T(8,128)(2,1)S(1)} %bitcast.82, pred[128,1152]{0,1:T(8,128)(4,1)S(1)} %bitcast_or_fusion, pred[8,1152]{1,0:T(8,128)(4,1)S(1)} %broadcast_bitcast_fusion), kind=kOutput, calls=%fused_computation.111 | convolution fusion | flops 306707456 | bytes 7500800 | tf_op jit(solution)/shard_map/zcs,zvs->zcv/dot_general | solution.py:56
  95.0 0.6 fusion.2
  95.7 1.3 fusion.19
  96.9 0.2 copy.83
  97.1 0.8 stack.19
  98.0 1.7 slice.48
  99.7 0.1 fusion.30
  99.8 2.5 %gather_fusion = bf16[72,128,128]{2,1,0:T(8,128)(2,1)} fusion(bf16[32,128,128]{2,1,0:T(8,128)(2,1)S(1)} %bitcast.69, s32[1024]{0:T(1024)S(1)} %pad_clamp_fusion.1), kind=kCustom, calls=%fused_computation.clone | custom fusion | bytes 4718880 | tf_op jit(solution)/shard_map/jit(_take)/gather | solution.py:50
  102.3 2.4 %gather_fusion.1 = bf16[72,128,128]{2,1,0:T(8,128)(2,1)} fusion(bf16[32,128,128]{2,1,0:T(8,128)(2,1)S(1)} %bitcast.68, s32[1024]{0:T(1024)S(1)} %pad_clamp_fusion.1), kind=kCustom, calls=%fused_computation.2.clone | custom fusion | bytes 4718880 | tf_op jit(solution)/shard_map/jit(_take)/gather | solution.py:53
  104.7 2.4 %broadcast_select_fusion.3 = (bf16[72,128,128]{2,1,0:T(8,128)(2,1)S(1)}, bf16[72,128,128]{2,1,0:T(8,128)(2,1)S(1)}) fusion(bf16[72,128,128]{2,1,0:T(8,128)(2,1)S(1)} %copy-done.3, pred[72]{0:T(512)(128)(4,1)S(1)} %get-tuple-element.57, bf16[72,128,128]{2,1,0:T(8,128)(2,1)} %gather_fusion.1), kind=kLoop, calls=%fused_computation.22 | loop fusion | flops 2359296 | bytes 9437256 | tf_op jit(solution)/shard_map/jit(_take)/select_n | solution.py:50
  107.1 2.9 %fusion.35 = (f32[8,128]{1,0:T(8,128)S(1)}, f32[8,128,1152]{1,2,0:T(8,128)S(1)}) fusion(bf16[8,1152,128]{2,1,0:T(8,128)(2,1)S(1)} %bitcast.75, bf16[8,128,128]{2,1,0:T(8,128)(2,1)S(1)} %bitcast.83, pred[128,1152]{0,1:T(8,128)(4,1)S(1)} %copy-done.8, pred[8,1152]{1,0:T(8,128)(4,1)S(1)} %broadcast_bitcast_fusion.1), kind=kOutput, calls=%fused_computation.112 | convolution fusion | flops 306707456 | bytes 7500800 | tf_op jit(solution)/shard_map/zcs,zvs->zcv/dot_general | solution.py:56
  110.1 0.6 fusion
  110.7 1.3 fusion.13
  112.0 0.2 copy.84
  112.2 0.1 stack.18
  112.3 0.1 maximum_bitcast_fusion
  112.4 10.2 %convolution_convert_fusion = bf16[512,8192]{1,0:T(8,128)(2,1)} fusion(bf16[512,512]{1,0:T(8,128)(2,1)S(1)} %bitcast.81, bf16[512,8192]{1,0:T(8,128)(2,1)} %param.14), kind=kOutput, calls=%fused_computation.4 | convolution fusion | flops 4299161600 | bytes 17301504 | tf_op jit(solution)/shard_map/dot_general | solution.py:125
  122.7 75.1 %reduce-scatter.2.cloned.1.call-done = bf16[32,8192]{1,0:T(8,128)(2,1)} async-done(((bf16[512,8192]{1,0:T(8,128)(2,1)}), bf16[32,8192]{1,0:T(8,128)(2,1)}) %reduce-scatter.2.cloned.1.call-update) | async-done | bytes 524304 | tf_op jit(solution)/shard_map/reduce_scatter | solution.py:124
  (40 shorter events, 0.3 us)
Async XLA Ops:
  6.5 11.8 %copy-start = (s32[64,4]{0,1:T(4,128)S(1)}, s32[64,4]{0,1:T(4,128)}, u32[]{:S(2)}) copy-start(s32[64,4]{0,1:T(4,128)} %param.17) | copy-start | bytes 3076
  10.6 7.7 %copy-start.10 = (s32[2,16]{1,0:T(2,128)S(1)}, s32[2,16]{1,0:T(2,128)}, u32[]{:S(2)}) copy-start(s32[2,16]{1,0:T(2,128)} %param.15) | copy-start | bytes 388
  10.6 9.8 %copy-start.9 = (s32[64,4]{0,1:T(4,128)S(1)}, s32[64,4]{0,1:T(4,128)}, u32[]{:S(2)}) copy-start(s32[64,4]{0,1:T(4,128)} %param.16) | copy-start | bytes 3076
  10.6 12.4 %copy-start.5 = (bf16[2,256,512]{2,1,0:T(8,128)(2,1)S(1)}, bf16[2,256,512]{2,1,0:T(8,128)(2,1)}, u32[]{:S(2)}) copy-start(bf16[2,256,512]{2,1,0:T(8,128)(2,1)} %param.11) | copy-start | bytes 1572868
  10.6 66.8 %all-to-all-start = ((bf16[16,2,2,256,128]{4,3,2,1,0:T(8,128)(2,1)}), bf16[16,2,2,256,128]{4,3,2,1,0:T(8,128)(2,1)}, u32[]{:S(2)}, u32[]{:S(2)}) async-start(bf16[16,2,2,256,128]{4,3,2,1,0:T(8,128)(2,1)} %stack.17), calls=%async_computation | async-start | bytes 8388608 | tf_op jit(solution)/shard_map/all_to_all | solution.py:92
  18.2 179.6 %reduce-scatter.2.cloned.1.call-start = ((), (), s32[]{:S(2)}) async-start(), calls=%async_computation.2 | async-start | bytes 8912896 | tf_op jit(solution)/shard_map/reduce_scatter | solution.py:124
  24.9 67.0 %copy-start.7 = (pred[128,1152]{0,1:T(8,128)(4,1)}, pred[128,1152]{0,1:T(8,128)(4,1)S(1)}, u32[]{:S(2)}) copy-start(pred[128,1152]{0,1:T(8,128)(4,1)S(1)} %bitcast_or_fusion) | copy-start | bytes 442372
  79.8 2.6 %copy-start.2 = (bf16[16,2,2,256,128]{4,3,0,2,1:T(8,128)(2,1)}, bf16[16,2,2,256,128]{4,3,0,2,1:T(8,128)(2,1)S(1)}, u32[]{:S(2)}) copy-start(bf16[16,2,2,256,128]{4,3,0,2,1:T(8,128)(2,1)S(1)} %copy.85) | copy-start | bytes 12582916
  102.3 2.4 %copy-start.3 = (bf16[72,128,128]{2,1,0:T(8,128)(2,1)S(1)}, bf16[72,128,128]{2,1,0:T(8,128)(2,1)}, u32[]{:S(2)}) copy-start(bf16[72,128,128]{2,1,0:T(8,128)(2,1)} %gather_fusion) | copy-start | bytes 7077892
  104.7 2.4 %copy-start.6 = (bf16[2,128,4,128]{3,1,0,2:T(8,128)(2,1)S(1)}, bf16[2,128,4,128]{3,1,0,2:T(8,128)(2,1)}, u32[]{:S(2)}) copy-start(bf16[2,128,4,128]{3,1,0,2:T(8,128)(2,1)} %copy.63) | copy-start | bytes 786436
  104.7 2.4 %copy-start.8 = (pred[128,1152]{0,1:T(8,128)(4,1)S(1)}, pred[128,1152]{0,1:T(8,128)(4,1)}, u32[]{:S(2)}) copy-start(pred[128,1152]{0,1:T(8,128)(4,1)} %copy-done.7) | copy-start | bytes 442372
  110.7 1.6 copy-start.4
  122.7 75.1 %copy-start.1 = (s32[64,4]{0,1:T(4,128)S(1)}, s32[64,4]{0,1:T(4,128)}, u32[]{:S(2)}) copy-start(s32[64,4]{0,1:T(4,128)} %param.17) | copy-start | bytes 3076
Sparse Core Ops, SparseCore 0:
  122.8 74.9 reduce-scatter.1
